TPU v7x, 512 devices: a whole 4x4x16 slice. The times are simulated.
512 devices in a mesh: dp: 16 (over z), seq: 8 (over x, core), index: 4 (over y).
Axes of the slice: x: 4, y: 4, z: 16, core: 2. Of those that a mesh axis runs over, the one named last changes fastest.
Arguments:
- hidden: bfloat16 [16, 2048, 2048], P('dp', 'seq'), may hold values from -32 to 32
- proj_weight: bfloat16 [4, 2048, 1536], P(None, 'dp', 'index')
- stretch_lengths: int32 [16, 32], P('dp'), may hold values from 1 to 512, 2048 in all within a row
- shard_of: int32 [16, 32, 1], P('dp', 'seq'), may hold values from 0 to 3; in each aligned block of 4 rows (0 to 3, 4 to 7, ..., all dimensions but the last counted through in order) at most 2 rows name the same one
Outputs:
- layer_out: bfloat16 [16, 2048, 2048], P('dp', 'seq', 'index')
- shelf: float32 [16, 8, 4, 2, 2048], P('dp', 'seq', 'index')
Inputs may be any that keep to these rules, and one draw needn't show every extreme that they name: `stretch_lengths`: the 32 lengths of a manual sum to 2048; the largest is 512. `shard_of`: in each aligned block of 4 rows of a manual no shard is named more than 2 times, a bound that some block reaches.
All inputs are finite; a program needn't handle non-finite values.
Results may differ from a plain program's by a relative error of at most 0.01.
Values may be sent and summed in bfloat16 or wider, within the bound.
A program may use at most 64 MiB of HBM per device.

v0:
```python
import jax
import jax.numpy as jnp
from jax import lax
from jax.sharding import PartitionSpec as P

D = 2048
HD = 64
HALF_WIN = 256


def with_halo(cells, sides, width):
    for axis, dim in sides:
        count = lax.axis_size(axis)
        ends = count - 1
        head = lax.slice_in_dim(cells, 0, width, axis=dim)
        tail = lax.slice_in_dim(cells, cells.shape[dim] - width, cells.shape[dim], axis=dim)
        cells = jnp.concatenate(
            [
                lax.ppermute(tail, axis, [(i, (i + 1) % count) for i in range(ends)]),
                cells,
                lax.ppermute(head, axis, [((i + 1) % count, i) for i in range(ends)]),
            ],
            axis=dim,
        )
    return cells


def rotate(values_in, positions):
    half_dim = HD // 2
    freqs = 10000.0 ** (-2.0 * jnp.arange(half_dim, dtype=jnp.float32) / HD)
    angles = positions.astype(jnp.float32)[:, None] * freqs[None, :]
    cosine = jnp.cos(angles)[:, None, :]
    sine = jnp.sin(angles)[:, None, :]
    first = values_in[..., :half_dim]
    second = values_in[..., half_dim:]
    return jnp.concatenate([first * cosine - second * sine, second * cosine + first * sine], -1)


def window_heads(queries, key_rows, value_rows, visible):
    scale = HD ** (-0.5)

    def one_head(items):
        query_head, key_head, value_head = items
        scores = jnp.dot(query_head, key_head.T, preferred_element_type=jnp.float32) * scale
        scores = jnp.where(visible, scores, -1e30)
        maxima = jnp.max(scores, -1, keepdims=True)
        expo = jnp.exp(scores - maxima)
        weights = (expo / jnp.sum(expo, -1, keepdims=True)).astype(jnp.bfloat16)
        return jnp.dot(weights, value_head, preferred_element_type=jnp.float32).astype(jnp.bfloat16)

    context = lax.map(
        one_head,
        (jnp.moveaxis(queries, 1, 0), jnp.moveaxis(key_rows, 1, 0), jnp.moveaxis(value_rows, 1, 0)),
    )
    return jnp.moveaxis(context, 0, 1)


def body(hidden, proj_weight, stretch_lengths, shard_of):
    states = hidden[0]
    tokens_here = states.shape[0]
    width = proj_weight.shape[2]
    heads_here = width // HD
    seq_index = lax.axis_index("seq")
    group_index = lax.axis_index("index")
    seq_count = lax.axis_size("seq")
    index_count = lax.axis_size("index")
    total_length = tokens_here * seq_count
    positions = seq_index * tokens_here + jnp.arange(tokens_here, dtype=jnp.int32)
    shard_rows = lax.all_gather(proj_weight, "dp", axis=1, tiled=True)
    projected = jnp.einsum(
        "td,jdc->jtc", states, shard_rows[:3], preferred_element_type=jnp.float32
    )
    out_rows_full = shard_rows[3]
    queries = rotate(projected[0].reshape(tokens_here, heads_here, HD), positions).astype(
        jnp.bfloat16
    )
    key_rows = rotate(projected[1].reshape(tokens_here, heads_here, HD), positions).astype(
        jnp.bfloat16
    )
    value_rows = projected[2].astype(jnp.bfloat16)
    stacked = jnp.stack([key_rows.reshape(tokens_here, width), value_rows])
    padded = with_halo(stacked, (("seq", 1),), HALF_WIN)
    span = tokens_here + 2 * HALF_WIN
    key_part = padded[0, 0:span].reshape(span, heads_here, HD)
    value_part = padded[1, 0:span].reshape(span, heads_here, HD)
    key_pos = seq_index * tokens_here + 0 - HALF_WIN + jnp.arange(span, dtype=jnp.int32)
    visible = (
        (jnp.abs(key_pos[None, :] - positions[:, None]) <= HALF_WIN)
        & (key_pos[None, :] >= 0)
        & (key_pos[None, :] < total_length)
    )
    context_parts = window_heads(queries, key_part, value_part, visible).reshape(tokens_here, width)
    partial_value = lax.dot_general(
        context_parts, out_rows_full, (((1,), (1,)), ((), ())), preferred_element_type=jnp.float32
    )
    lengths = stretch_lengths[0]
    stretch_count = lengths.shape[0]
    per_block = stretch_count // seq_count
    ends = jnp.cumsum(lengths, dtype=jnp.int32)
    starts = ends - lengths
    row_ids = jnp.arange(stretch_count, dtype=jnp.int32)
    order = row_ids % per_block * seq_count + row_ids // per_block
    row_starts = starts[order]
    row_ends = ends[order]
    member = (
        (positions[None, :] >= row_starts[:, None]) & (positions[None, :] < row_ends[:, None])
    ).astype(jnp.bfloat16)
    shard_ids = shard_of[0, :, 0]
    local_rows = jnp.arange(per_block, dtype=jnp.int32)
    earlier = (shard_ids[:, None] == shard_ids[None, :]) & (
        local_rows[None, :] < local_rows[:, None]
    )
    slot_rank = jnp.sum(earlier.astype(jnp.int32), 1)
    capacity = per_block // 2
    slot_ids = jnp.arange(capacity, dtype=jnp.int32)
    quarter = D // index_count
    summed = lax.psum_scatter(
        partial_value.astype(jnp.bfloat16), "index", scatter_dimension=1, tiled=True
    ).astype(jnp.float32)
    own_states = lax.dynamic_slice_in_dim(states, group_index * quarter, quarter, 1)
    layer = (own_states.astype(jnp.float32) + summed).astype(jnp.bfloat16)
    partial_pool = jnp.dot(member, layer, preferred_element_type=jnp.float32)
    pooled = lax.psum_scatter(
        partial_pool.astype(jnp.bfloat16), "seq", scatter_dimension=0, tiled=True
    ).astype(jnp.float32)
    shard_range = jnp.arange(index_count, dtype=jnp.int32)
    routing = (
        (shard_ids[None, None, :] == shard_range[:, None, None])
        & (slot_rank[None, None, :] == slot_ids[None, :, None])
    ).astype(jnp.float32)
    outgoing = jnp.einsum("rkc,cf->rkf", routing, pooled, precision=lax.Precision.HIGHEST)
    arrived = lax.all_to_all(outgoing, "index", split_axis=0, concat_axis=2, tiled=True)[0]
    shelf_rows = arrived * lax.rsqrt(jnp.mean(arrived * arrived, -1, keepdims=True) + 1e-06)
    return (layer[None], shelf_rows[None, None, None])


def solution(mesh):
    in_specs = (P("dp", "seq", None), P(None, "dp", "index"), P("dp", None), P("dp", "seq", None))
    out_specs = (P("dp", "seq", "index"), P("dp", "seq", "index", None, None))
    return jax.shard_map(body, mesh=mesh, in_specs=in_specs, out_specs=out_specs, check_vma=False)
```

profile of v0, /device:TPU:32, one launch (start us, length us, event | category | flops | bytes accessed | tf_op | source)
XLA Modules:
  0.0 226.8 jit_solution(12025470082465413667)
XLA Ops:
  7.2 0.0 all-gather.2.cloned.1.call-start
  7.2 1.9 copy.24
  9.2 0.0 all-gather.2.cloned.1.call-update
  9.2 0.0 reduce-scatter.2.cloned.1.call-start
  9.3 1.2 multiply_cosine_fusion
  10.5 116.8 %all-gather.2.cloned.1.call-done = bf16[4,2048,384]{1,2,0:T(8,128)(2,1)} async-done(((bf16[4,128,384]{1,2,0:T(8,128)(2,1)}), bf16[4,2048,384]{1,2,0:T(8,128)(2,1)}) %all-gather.2.cloned.1.call-update) | async-done | bytes 6291472 | tf_op jit(solution)/shard_map/all_gather | solution.py:69
  127.3 4.1 %convolution_bitcast_fusion = f32[3,256,384]{1,2,0:T(8,128)S(1)} fusion(bf16[4,2048,384]{1,2,0:T(8,128)(2,1)} %all-gather.2.cloned.1.call-done, bf16[1,256,2048]{2,1,0:T(8,128)(2,1)} %param.6), kind=kOutput, calls=%fused_computation.24 | convolution fusion | flops 1207959552 | bytes 8519680 | tf_op jit(solution)/shard_map/td,jdc->jtc/dot_general | solution.py:70
  131.4 0.1 fusion.40
  131.6 0.3 copy.39
  131.8 0.3 copy.37
  132.1 0.3 copy.38
  132.4 0.3 copy.36
  132.6 1.4 subtract_convert_fusion
  134.1 0.4 maximum_bitcast_fusion
  134.5 0.2 copy.29
  134.7 1.3 collective-permute-start.1
  136.0 3.1 %collective-permute-start = (bf16[2,256,384]{1,2,0:T(8,128)(2,1)S(1)}, bf16[2,256,384]{1,2,0:T(8,128)(2,1)S(1)}, u32[]{:S(2)}, u32[]{:S(2)}) collective-permute-start(bf16[2,256,384]{1,2,0:T(8,128)(2,1)S(1)} %pad_maximum_fusion.2), channel_id=1, source_target_pairs={{0,4},{4,8},{8,12},{12,16},{16,20},{20,24},{24,28},{1,5},{5,9},{9,... | collective-permute-start | bytes 1179656 | tf_op jit(solution)/shard_map/ppermute | solution.py:19
  139.1 0.0 collective-permute-done.1
  139.1 1.2 collective-permute-done
  140.4 0.1 pad_maximum_fusion
  140.5 0.1 fusion.39
  140.6 0.7 copy.30
  141.3 0.7 copy.31
  142.0 7.3 %while.11 = (s32[]{:T(128)}, bf16[6,256,64]{1,2,0:T(8,128)(2,1)S(1)}, bf16[6,256,64]{2,1,0:T(8,128)(2,1)S(1)}, bf16[6,768,64]{2,1,0:T(8,128)(2,1)S(1)}, bf16[6,7...) while((s32[]{:T(128)}, ...), condition=%wide.region_3.4_spmd.clone, body=%wide.region_0.3_spmd.clone.sunk | while | flops 52903424 | bytes 2865261 | solution.py:51
  142.0 0.5 fusion.50
  142.6 0.3 fusion.51
  142.9 0.4 fusion.52
  143.2 0.5 fusion.50
  143.8 0.3 fusion.51
  144.1 0.4 fusion.52
  144.5 0.5 fusion.50
  145.0 0.3 fusion.51
  145.3 0.4 fusion.52
  145.7 0.5 fusion.50
  146.2 0.3 fusion.51
  146.5 0.4 fusion.52
  146.9 0.5 fusion.50
  147.4 0.3 fusion.51
  147.7 0.4 fusion.52
  148.1 0.5 fusion.50
  148.6 0.3 fusion.51
  148.9 0.4 fusion.52
  149.3 0.0 copy-start.1
  149.3 3.2 %convolution_convert_fusion.1 = bf16[256,2048]{1,0:T(8,128)(2,1)} fusion(bf16[256,384]{0,1:T(8,128)(2,1)S(1)} %bitcast.86, bf16[4,2048,384]{1,2,0:T(8,128)(2,1)} %all-gather.2.cloned.1.call-done), kind=kOutput, calls=%fused_computation.22 | convolution fusion | flops 403177472 | bytes 2818048 | tf_op jit(solution)/shard_map/dot_general | solution.py:93
  152.5 0.0 reduce-scatter.2.cloned.1.call-update
  152.5 0.0 copy-done.1
  152.5 0.1 copy.32
  152.6 0.1 reduce-window.9
  152.7 0.1 reduce.1
  152.8 0.7 gather_fusion.1
  153.5 0.7 gather_fusion
  154.2 1.3 dynamic-slice.1
  156.2 0.0 copy-done.2
  156.2 0.2 convert_reduce_fusion
  156.4 28.2 %reduce-scatter.2.cloned.1.call-done = bf16[256,512]{1,0:T(8,128)(2,1)} async-done(((bf16[256,2048]{1,0:T(8,128)(2,1)}), bf16[256,512]{1,0:T(8,128)(2,1)}) %reduce-scatter.2.cloned.1.call-update) | async-done | bytes 262160 | tf_op jit(solution)/shard_map/reduce_scatter | solution.py:117
  184.6 0.0 copy-done
  184.6 1.1 convolution_convert_fusion.2
  185.7 24.1 %all-reduce = bf16[32,512]{1,0:T(8,128)(2,1)S(1)} all-reduce(bf16[32,512]{1,0:T(8,128)(2,1)S(1)} %convolution_convert_fusion.2), channel_id=3, replica_groups=mesh['dp'=16,'seq'=8,'index'=4] {'seq'}, use_global_device_ids=true, to_apply=%region_7.8.clone | all-reduce | flops 16384 | bytes 65536
  209.8 0.7 fusion.27
  210.6 3.3 %all-to-all-start = ((f32[4,2,512]{2,1,0:T(2,128)}), f32[4,2,512]{2,1,0:T(2,128)S(1)}, u32[]{:S(2)}, u32[]{:S(2)}) async-start(f32[4,2,512]{2,1,0:T(2,128)} %fusion.27), calls=%async_computation.1 | async-start | bytes 32768 | tf_op jit(solution)/shard_map/all_to_all | solution.py:132
  213.8 1.7 fusion.19
  215.6 3.6 %all-to-all-done = f32[4,2,512]{2,1,0:T(2,128)S(1)} async-done(((f32[4,2,512]{2,1,0:T(2,128)}), f32[4,2,512]{2,1,0:T(2,128)S(1)}, u32[]{:S(2)}, u32[]{:S(2)}) %all-to-all-start) | async-done | bytes 16416 | tf_op jit(solution)/shard_map/all_to_all | solution.py:132
  219.2 0.1 fusion.23
  219.3 0.7 broadcast_multiply_fusion
  (19 shorter events, 0.2 us)
Async XLA Ops:
  7.2 120.1 %all-gather.2.cloned.1.call-start = ((), (), s32[]{:S(2)}) async-start(), calls=%async_computation.2 | async-start | bytes 6684672 | tf_op jit(solution)/shard_map/all_gather | solution.py:69
  9.2 175.4 %reduce-scatter.2.cloned.1.call-start = ((), (), s32[]{:S(2)}) async-start(), calls=%async_computation.3 | async-start | bytes 1310720 | tf_op jit(solution)/shard_map/reduce_scatter | solution.py:117
  134.7 4.4 %collective-permute-start.1 = (bf16[2,256,384]{1,2,0:T(8,128)(2,1)S(1)}, bf16[2,256,384]{1,2,0:T(8,128)(2,1)S(1)}, u32[]{:S(2)}, u32[]{:S(2)}) collective-permute-start(bf16[2,256,384]{1,2,0:T(8,128)(2,1)S(1)} %pad_maximum_fusion.2), channel_id=1, source_target_pairs={{4,0},{8,4},{12,8},{16,12},{20,16},{24,20},{28,24},{5,1},{9,5},{13... | collective-permute-start | bytes 1179656 | tf_op jit(solution)/shard_map/ppermute | solution.py:21
  136.0 4.4 %collective-permute-start = (bf16[2,256,384]{1,2,0:T(8,128)(2,1)S(1)}, bf16[2,256,384]{1,2,0:T(8,128)(2,1)S(1)}, u32[]{:S(2)}, u32[]{:S(2)}) collective-permute-start(bf16[2,256,384]{1,2,0:T(8,128)(2,1)S(1)} %pad_maximum_fusion.2), channel_id=1, source_target_pairs={{0,4},{4,8},{8,12},{12,16},{16,20},{20,24},{24,28},{1,5},{5,9},{9,... | collective-permute-start | bytes 1179656 | tf_op jit(solution)/shard_map/ppermute | solution.py:19
  149.3 3.2 %copy-start.1 = (s32[1,32]{1,0:T(1,128)S(1)}, s32[1,32]{1,0:T(1,128)}, u32[]{:S(2)}) copy-start(s32[1,32]{1,0:T(1,128)} %param.8) | copy-start | bytes 388
  152.5 3.7 %copy-start.2 = (s32[1,4,1]{1,2,0:T(1,128)S(1)}, s32[1,4,1]{1,2,0:T(1,128)}, u32[]{:S(2)}) copy-start(s32[1,4,1]{1,2,0:T(1,128)} %param.9) | copy-start | bytes 52
  152.5 32.1 %copy-start = (bf16[1,256,2048]{2,1,0:T(8,128)(2,1)S(1)}, bf16[1,256,2048]{2,1,0:T(8,128)(2,1)}, u32[]{:S(2)}) copy-start(bf16[1,256,2048]{2,1,0:T(8,128)(2,1)} %param.6) | copy-start | bytes 3145732
  210.6 8.6 %all-to-all-start = ((f32[4,2,512]{2,1,0:T(2,128)}), f32[4,2,512]{2,1,0:T(2,128)S(1)}, u32[]{:S(2)}, u32[]{:S(2)}) async-start(f32[4,2,512]{2,1,0:T(2,128)} %fusion.27), calls=%async_computation.1 | async-start | bytes 32768 | tf_op jit(solution)/shard_map/all_to_all | solution.py:132
Sparse Core Ops, SparseCore 0:
  10.0 117.2 all-gather.1
  152.6 31.8 reduce-scatter.1
where the time goes:
time: 227 us
  waiting for transfers between devices  150 us (66%)
  blocking collectives  24.1 us (11%)
  between operations  15 us (7%)
  matrix products  14.7 us (6%)
  other arithmetic  7.88 us (3%)
  starting transfers between devices  7.68 us (3%)
  local copies, waits for them, and re-layouts  7.61 us (3%)
    all_gather x1, waiting for transfers between devices, body(): shard_rows = lax.all_gather(proj_weight, 'dp', axis=1, tiled=True)  117 us
    reduce_scatter x1, waiting for transfers between devices, body(): lax.psum_scatter(partial_value.astype(jnp.bfloat16), 'index', scatter_dim...  28.2 us
    unnamed x1, blocking collectives  24.1 us
  transfers between devices with their start and end apart: 5, of which 4 were waited for; matrix products, arithmetic and copies ran while one was open for 3% of the time, Pallas kernels for 0%

commit v1 on v0

--- a/solution.py
+++ b/solution.py
@@ -66,7 +66,9 @@
     index_count = lax.axis_size("index")
     total_length = tokens_here * seq_count
     positions = seq_index * tokens_here + jnp.arange(tokens_here, dtype=jnp.int32)
-    shard_rows = lax.all_gather(proj_weight, "dp", axis=1, tiled=True)
+    shard_rows = jnp.concatenate(
+        lax.all_to_all(jnp.stack([proj_weight] * lax.axis_size("dp")), "dp", 0, 0), axis=1
+    )
     projected = jnp.einsum(
         "td,jdc->jtc", states, shard_rows[:3], preferred_element_type=jnp.float32
     )

time: 227 us -> 420 us (1.85)
  waiting for transfers between devices: 150 us -> 308 us
  local copies, waits for them, and re-layouts: 7.61 us -> 24.9 us
  starting transfers between devices: 7.68 us -> 21.1 us
    all_to_all x0 -> x1, waiting for transfers between devices: none -> 272 us  [body(): lax.all_to_all(jnp.stack([proj_weight] * lax.axis_size('dp')), 'dp', 0, 0)]
    all_gather x1 -> x0, waiting for transfers between devices: 117 us -> none  [body(): shard_rows = lax.all_gather(proj_weight, 'dp', axis=1, tiled=True)]
    all_to_all x0 -> x1, starting transfers between devices: none -> 15.2 us  [body(): lax.all_to_all(jnp.stack([proj_weight] * lax.axis_size('dp')), 'dp', 0, 0)]
    all_to_all x0 -> x1, local copies, waits for them, and re-layouts: none -> 8.66 us  [body(): lax.all_to_all(jnp.stack([proj_weight] * lax.axis_size('dp')), 'dp', 0, 0)]
    dot_general x6, matrix products: 3.23 us -> 9 us  [one_head(): jnp.dot(query_head, key_head.T, preferred_element_type=jnp.float32) * scale]
    slice x0 -> x2, local copies, waits for them, and re-layouts: none -> 4.57 us  [the longest x1 2.9 us: body(): shard_rows[:3]]
  transfers between devices with their start and end apart: 5 -> 5, of which waited for: 4 -> 4; matrix products, arithmetic and copies ran while one was open for 3% -> 2% of each run, Pallas kernels for 0% -> 0%
where the time goes in v1:
time: 420 us; the launch traced here: 419 us
  waiting for transfers between devices  308 us (73%)
  local copies, waits for them, and re-layouts  24.9 us (6%)
  blocking collectives  24 us (6%)
  starting transfers between devices  21.1 us (5%)
  matrix products  16.4 us (4%)
  between operations  15 us (4%)
  other arithmetic  9.51 us (2%)
    all_to_all x1, waiting for transfers between devices, body(): lax.all_to_all(jnp.stack([proj_weight] * lax.axis_size('dp')), 'dp', 0, 0)  272 us
    reduce_scatter x1, waiting for transfers between devices, body(): lax.psum_scatter(partial_value.astype(jnp.bfloat16), 'index', scatter_dim...  31.8 us
    unnamed x1, blocking collectives  24 us
    all_to_all x1, starting transfers between devices, body(): lax.all_to_all(jnp.stack([proj_weight] * lax.axis_size('dp')), 'dp', 0, 0)  15.2 us
    dot_general x6, matrix products, one_head(): jnp.dot(query_head, key_head.T, preferred_element_type=jnp.float32) * scale  9 us
    all_to_all x1, local copies, waits for them, and re-layouts, body(): lax.all_to_all(jnp.stack([proj_weight] * lax.axis_size('dp')), 'dp', 0, 0)  8.66 us
  transfers between devices with their start and end apart: 5, of which 4 were waited for; matrix products, arithmetic and copies ran while one was open for 2% of the time, Pallas kernels for 0%

profile of v1, /device:TPU:32, one launch (start us, length us, event | category | flops | bytes accessed | tf_op | source)
XLA Modules:
  0.0 419.3 jit_solution(1898351370210237286)
XLA Ops:
  7.2 1.2 copy.35
  8.4 4.2 stack.4
  12.6 15.2 %all-to-all-start = ((bf16[16,4,128,384]{2,3,1,0:T(8,128)(2,1)}), bf16[16,4,128,384]{2,3,1,0:T(8,128)(2,1)}, u32[]{:S(2)}, u32[]{:S(2)}) async-start(bf16[16,4,128,384]{2,3,1,0:T(8,128)(2,1)} %stack.4), calls=%async_computation | async-start | bytes 12582912 | tf_op jit(solution)/shard_map/all_to_all | solution.py:70
  27.8 0.0 reduce-scatter.2.cloned.1.call-start
  27.8 1.2 multiply_cosine_fusion
  29.1 271.7 %all-to-all-done = bf16[16,4,128,384]{2,3,1,0:T(8,128)(2,1)} async-done(((bf16[16,4,128,384]{2,3,1,0:T(8,128)(2,1)}), bf16[16,4,128,384]{2,3,1,0:T(8,128)(2,1)}, u32[]{:S(2)}, u32[]{:S(2)}) %all-to-all-start) | async-done | bytes 6291488 | tf_op jit(solution)/shard_map/all_to_all | solution.py:70
  300.7 8.7 %copy.36 = bf16[16,4,128,384]{3,2,0,1:T(8,128)(2,1)} copy(bf16[16,4,128,384]{2,3,1,0:T(8,128)(2,1)} %all-to-all-done) | data formatting | bytes 12582912 | tf_op jit(solution)/shard_map/all_to_all | solution.py:70
  309.4 2.9 slice.54
  312.3 1.4 convolution_bitcast_fusion
  313.8 0.1 fusion.40
  313.9 0.3 copy.50
  314.2 0.3 copy.51
  314.5 0.3 copy.52
  314.8 0.3 copy.53
  315.0 2.3 subtract_convert_fusion
  317.3 0.2 pad_maximum_fusion.1
  317.5 0.2 copy.42
  317.8 1.3 collective-permute-start
  319.1 1.3 collective-permute-start.1
  320.4 1.7 slice.64
  322.1 1.0 maximum_bitcast_fusion
  323.1 1.3 collective-permute-done.1
  324.4 0.1 pad_maximum_fusion
  324.5 0.1 fusion.39
  324.6 1.4 copy.43
  325.9 0.7 copy.44
  326.7 13.0 %while.11 = (s32[]{:T(128)}, bf16[6,256,64]{1,2,0:T(8,128)(2,1)S(1)}, bf16[6,256,64]{2,1,0:T(8,128)(2,1)}, bf16[6,768,64]{2,1,0:T(8,128)(2,1)}, bf16[6,768,64]{2...) while((s32[]{:T(128)}, ...), condition=%wide.region_3.4_spmd.clone, body=%wide.region_0.3_spmd.clone.sunk | while | flops 52903424 | bytes 2863717 | solution.py:51
  326.7 1.5 fusion.51
  328.2 0.3 fusion.52
  328.4 0.4 fusion.53
  328.8 1.5 fusion.51
  330.3 0.3 fusion.52
  330.6 0.4 fusion.53
  331.0 1.5 fusion.51
  332.5 0.3 fusion.52
  332.8 0.4 fusion.53
  333.2 1.5 fusion.51
  334.7 0.3 fusion.52
  335.0 0.4 fusion.53
  335.4 1.5 fusion.51
  336.9 0.3 fusion.52
  337.1 0.4 fusion.53
  337.5 1.5 fusion.51
  339.0 0.3 fusion.52
  339.3 0.4 fusion.53
  339.7 0.0 copy-start.4
  339.7 1.7 convolution_convert_fusion.1
  341.5 0.0 reduce-scatter.2.cloned.1.call-update
  341.5 0.1 copy.45
  341.6 0.1 reduce-window.9
  341.7 0.1 reduce.1
  341.8 0.7 gather_fusion.1
  342.5 0.7 gather_fusion
  343.2 1.3 dynamic-slice.1
  345.1 0.2 convert_reduce_fusion
  345.4 31.8 %reduce-scatter.2.cloned.1.call-done = bf16[256,512]{1,0:T(8,128)(2,1)} async-done(((bf16[256,2048]{1,0:T(8,128)(2,1)}), bf16[256,512]{1,0:T(8,128)(2,1)}) %reduce-scatter.2.cloned.1.call-update) | async-done | bytes 262160 | tf_op jit(solution)/shard_map/reduce_scatter | solution.py:119
  377.2 1.1 convolution_convert_fusion.2
  378.3 24.0 %all-reduce = bf16[32,512]{1,0:T(8,128)(2,1)S(1)} all-reduce(bf16[32,512]{1,0:T(8,128)(2,1)S(1)} %convolution_convert_fusion.2), channel_id=3, replica_groups=mesh['dp'=16,'seq'=8,'index'=4] {'seq'}, use_global_device_ids=true, to_apply=%region_7.8.clone | all-reduce | flops 16384 | bytes 65536
  402.3 0.7 fusion.27
  403.1 3.3 all-to-all-start.1
  406.3 1.7 fusion.19
  408.1 3.6 all-to-all-done.1
  411.7 0.1 fusion.23
  411.8 0.7 broadcast_multiply_fusion
  (28 shorter events, 0.2 us)
Async XLA Ops:
  12.6 288.2 %all-to-all-start = ((bf16[16,4,128,384]{2,3,1,0:T(8,128)(2,1)}), bf16[16,4,128,384]{2,3,1,0:T(8,128)(2,1)}, u32[]{:S(2)}, u32[]{:S(2)}) async-start(bf16[16,4,128,384]{2,3,1,0:T(8,128)(2,1)} %stack.4), calls=%async_computation | async-start | bytes 12582912 | tf_op jit(solution)/shard_map/all_to_all | solution.py:70
  27.8 349.4 %reduce-scatter.2.cloned.1.call-start = ((), (), s32[]{:S(2)}) async-start(), calls=%async_computation.3 | async-start | bytes 1310720 | tf_op jit(solution)/shard_map/reduce_scatter | solution.py:119
  309.4 2.9 copy-start.2
  317.8 5.4 %collective-permute-start = (bf16[2,256,384]{1,2,0:T(8,128)(2,1)S(1)}, bf16[2,256,384]{1,2,0:T(8,128)(2,1)S(1)}, u32[]{:S(2)}, u32[]{:S(2)}) collective-permute-start(bf16[2,256,384]{1,2,0:T(8,128)(2,1)S(1)} %pad_maximum_fusion.2), channel_id=1, source_target_pairs={{0,4},{4,8},{8,12},{12,16},{16,20},{20,24},{24,28},{1,5},{5,9},{9,... | collective-permute-start | bytes 1179656 | tf_op jit(solution)/shard_map/ppermute | solution.py:19
  319.1 5.3 %collective-permute-start.1 = (bf16[2,256,384]{1,2,0:T(8,128)(2,1)S(1)}, bf16[2,256,384]{1,2,0:T(8,128)(2,1)S(1)}, u32[]{:S(2)}, u32[]{:S(2)}) collective-permute-start(bf16[2,256,384]{1,2,0:T(8,128)(2,1)S(1)} %pad_maximum_fusion.2), channel_id=1, source_target_pairs={{4,0},{8,4},{12,8},{16,12},{20,16},{24,20},{28,24},{5,1},{9,5},{13... | collective-permute-start | bytes 1179656 | tf_op jit(solution)/shard_map/ppermute | solution.py:21
  320.4 1.7 copy-start
  320.4 1.7 copy-start.1
  339.7 1.8 copy-start.4
  341.5 3.7 copy-start.5
  341.5 35.7 %copy-start.3 = (bf16[1,256,2048]{2,1,0:T(8,128)(2,1)S(1)}, bf16[1,256,2048]{2,1,0:T(8,128)(2,1)}, u32[]{:S(2)}) copy-start(bf16[1,256,2048]{2,1,0:T(8,128)(2,1)} %param.6) | copy-start | bytes 3145732
  403.1 8.6 %all-to-all-start.1 = ((f32[4,2,512]{2,1,0:T(2,128)}), f32[4,2,512]{2,1,0:T(2,128)S(1)}, u32[]{:S(2)}, u32[]{:S(2)}) async-start(f32[4,2,512]{2,1,0:T(2,128)} %fusion.27), calls=%async_computation.2 | async-start | bytes 32768 | tf_op jit(solution)/shard_map/all_to_all | solution.py:134
Sparse Core Ops, SparseCore 0:
  341.6 35.5 reduce-scatter.1
